TPU v7x, 128 devices: a whole 4x4x4 slice. The times are simulated.
128 devices in a mesh: vc: 8 (over x, y_hi), op: 16 (over y_lo, z, core).
Axes of the slice: x: 4, y: 4 (y_hi: 2, y_lo: 2; y = y_hi * 2 + y_lo), z: 4, core: 2. Of those that a mesh axis runs over, the one named last changes fastest.
Arguments:
- integrals: float32 [1024, 32768], P('op', 'vc'), may hold values from -0.046875 to 0.046875
- amplitudes: float32 [32768, 16384], P('vc', 'op'), may hold values from -6 to 6
- vir_energy: float32 [1024], P('vc'), may hold values from 1 to 10
- occ_energy: float32 [16384], P('op'), may hold values from -4 to -0.5
Outputs:
- update: float32 [1024, 16384], P('vc', 'op')
All inputs are finite; a program needn't handle non-finite values.
Results may differ from a plain program's by a relative error of at most 0.000076.
Values sent between devices are 32-bit elements; how exact they have to be, the bound alone decides.
A program may use at most 128 MiB of HBM per device.

v0:
```python
import jax
import jax.numpy as jnp
from jax import lax
from jax.experimental import pallas as pl
from jax.experimental.pallas import tpu as pltpu
from jax.sharding import PartitionSpec as P

MESH = pl.DeviceIdType.MESH
OFF = (0, 2560)
SIZE = (2560, 1536)
DEPTH = 4096
CHUNK = 1024
HALF = 32
BLOCK = 64
ROWS = 128
COLS = 1024
STRIP = 16
STAGE = 256
BUFS = 4
SLOTS = 8

OWN = (0, 0)
FULL, TOP, LOW = (0, 32), (0, 16), (16, 16)
SPLIT = (TOP, LOW)


def slot_of(place):
    return place[0] * 4 + place[1]


NEAR = [(1, 0), (0, 1), (0, 3)]
ARRIVALS = [[(place, h, t, (FULL,)) for place in NEAR] for h in (0, 1) for t in (0, 1)] + [
    [((1, 1), 0, 1, (FULL,)), ((1, 1), 0, 0, (FULL,)), ((1, 3), 0, 0, (FULL,))],
    [((1, 3), 0, 1, (FULL,)), ((0, 2), 0, 1, (FULL,)), ((1, 1), 1, 1, (FULL,))],
    [((1, 1), 1, 0, (FULL,)), ((1, 3), 1, 1, (FULL,))],
    [((1, 3), 1, 0, (FULL,)), ((0, 2), 1, 1, (FULL,))],
    [((1, 2), 0, 1, (FULL,)), ((1, 2), 0, 0, SPLIT)],
    [((0, 2), 0, 0, SPLIT), ((1, 2), 1, 1, (FULL,))],
    [((0, 2), 1, 0, SPLIT)],
    [((1, 2), 1, 0, SPLIT)],
]
RELAYS = {
    1: [("z+", (1, 0), 0, 0, FULL, (1, 3)), ("z-", (1, 0), 0, 0, FULL, (1, 1)),
        ("y", (0, 1), 0, 1, FULL, (1, 1))],
    2: [("z+", (0, 3), 0, 1, FULL, (0, 2)), ("z-", (1, 0), 1, 0, FULL, (1, 1)),
        ("y", (0, 3), 0, 1, FULL, (1, 3))],
    3: [("z+", (1, 0), 1, 0, FULL, (1, 3)), ("z-", (0, 1), 1, 1, FULL, (0, 2)),
        ("y", (0, 1), 1, 1, FULL, (1, 1)), ("y", (0, 3), 1, 1, FULL, (1, 3))],
    4: [("z+", (1, 3), 0, 0, TOP, (1, 2)), ("z-", (1, 1), 0, 0, LOW, (1, 2)),
        ("z+", (0, 3), 0, 0, TOP, (0, 2)), ("z-", (0, 1), 0, 0, LOW, (0, 2)),
        ("z+", (0, 3), 1, 0, TOP, (0, 2)), ("z-", (0, 1), 1, 0, LOW, (0, 2))],
    5: [("y", (0, 2), 0, 1, FULL, (1, 2))],
    6: [("z-", (1, 1), 1, 0, LOW, (1, 2))],
    7: [("z+", (1, 3), 1, 0, TOP, (1, 2)), ("y", (0, 2), 1, 1, FULL, (1, 2))],
}


def halves(half, *places):
    return [(place, half) for place in places]


SUM_X = {
    1: [(OWN, 0), (OWN, 1)],
    3: halves(0, *NEAR),
    6: halves(1, *NEAR),
    7: halves(0, (1, 1), (1, 3)),
    9: halves(1, (1, 1)),
    10: [((1, 3), 1), ((1, 2), 0)],
}
SUM_Y = {
    3: [(OWN, 0), (OWN, 1)],
    6: halves(0, *NEAR),
    9: halves(1, *NEAR),
    10: halves(0, (1, 1), (1, 3)),
}


def kernel(
    i_hbm, t_hbm, o_ref,
    got, thi, tlo, stage, part, rx, ry, st, ob, both,
    stage_sem, own_sem, send_sem, recv_sem, fwd_sem, sib_sem,
    xs_sem, xr_sem, ys_sem, yr_sem, os_sem, or_sem,
):
    vc, op = lax.axis_index("vc"), lax.axis_index("op")
    x, yh = vc // 2, vc % 2
    yl, z, core = op // 8, (op // 2) % 4, op % 2

    def at(x_, yh_, yl_, z_, core_):
        return {"vc": x_ * 2 + yh_, "op": yl_ * 8 + z_ * 2 + core_}

    to = {
        "z+": at(x, yh, yl, (z + 1) % 4, core),
        "z-": at(x, yh, yl, (z + 3) % 4, core),
        "y": at(x, yh, 1 - yl, z, core),
        "c": at(x, yh, yl, z, 1 - core),
    }
    opposite = at(x, 1 - yh, yl, z, core)

    def stage_copy(s):
        return pltpu.make_async_copy(
            t_hbm.at[pl.ds(s * STAGE, STAGE)],
            stage.at[s % BUFS],
            stage_sem.at[s % BUFS],
        )

    for s in range(BUFS):
        stage_copy(s).start()

    first = pl.multiple_of(core * HALF, HALF)

    mine = [
        pltpu.make_async_copy(
            i_hbm.at[pl.ds(h * HALF, HALF)],
            got.at[0, pl.ds(pl.multiple_of(h * BLOCK + first, HALF), HALF)],
            own_sem.at[h],
        )
        for h in (0, 1)
    ]
    for copy in mine:
        copy.start()

    barrier = pltpu.get_barrier_semaphore()
    partners = list(to.values()) + [opposite]
    partners += [at((x + d) % 4, yh, yl, z, core) for d in (1, 2, 3)]
    for partner in partners:
        pl.semaphore_signal(barrier, inc=1, device_id=partner, device_id_type=MESH)
    pl.semaphore_wait(barrier, len(partners))

    started = []
    counts = {"send": 0, "fwd": 0}

    def window(place, half, part_, base, rows):
        start = pl.multiple_of(half * BLOCK + base + rows[0], STRIP)
        return got.at[slot_of(place), pl.ds(start, rows[1]), pl.ds(OFF[part_], SIZE[part_])]

    def which(half, part_, rows):
        return half * 4 + part_ * 2 + (1 if rows == LOW else 0)

    def send(src, link, place, half, part_, rows):
        copy = pltpu.make_async_remote_copy(
            src_ref=src,
            dst_ref=window(place, half, part_, first, rows),
            send_sem=send_sem.at[counts["send"]],
            recv_sem=recv_sem.at[slot_of(place), which(half, part_, rows)],
            device_id=to[link],
            device_id_type=MESH,
        )
        counts["send"] += 1
        copy.start()
        started.append(copy)

    def forward(src, dst, sem):
        copy = pltpu.make_async_remote_copy(
            src_ref=src,
            dst_ref=dst,
            send_sem=fwd_sem.at[counts["fwd"]],
            recv_sem=sem,
            device_id=to["c"],
            device_id_type=MESH,
        )
        counts["fwd"] += 1
        copy.start()
        started.append(copy)

    def arrival(ref, sem):
        pltpu.make_async_remote_copy(
            src_ref=ref,
            dst_ref=ref,
            send_sem=send_sem.at[0],
            recv_sem=sem,
            device_id=to["c"],
            device_id_type=MESH,
        ).wait_recv()

    def arrived(sem, place, half, part_, base, rows):
        arrival(
            window(place, half, part_, base, rows),
            sem.at[slot_of(place), which(half, part_, rows)],
        )

    for h in (0, 1):
        for t in (0, 1):
            src = i_hbm.at[pl.ds(h * HALF, HALF), pl.ds(OFF[t], SIZE[t])]
            for link, place in (("y", (1, 0)), ("z+", (0, 3)), ("z-", (0, 1))):
                send(src, link, place, h, t, FULL)
        rows = pl.ds(pl.multiple_of(h * BLOCK + first, HALF), HALF)
        forward(i_hbm.at[pl.ds(h * HALF, HALF)], got.at[0, rows], sib_sem.at[0, h])

    def split_stage(s):
        stage_copy(s).wait()

        @pl.loop(0, STAGE // 64)
        def _(k):
            rows = pl.ds(pl.multiple_of(k * 64, 64), 64)
            into = pl.ds(pl.multiple_of(s * STAGE + k * 64, 64), 64)
            v = stage[s % BUFS, rows, :]
            h = v.astype(jnp.bfloat16)
            thi[into, :] = h
            tlo[into, :] = (v - h.astype(jnp.float32)).astype(jnp.bfloat16)

        if s + BUFS < DEPTH // STAGE:
            stage_copy(s + BUFS).start()

    def x_copy(slot, half, k):
        other = (x + k) % 4
        start = pl.multiple_of(half * BLOCK + other * STRIP, STRIP)
        return pltpu.make_async_remote_copy(
            src_ref=part.at[slot, pl.ds(start, STRIP)],
            dst_ref=rx.at[slot, half, k - 1],
            send_sem=xs_sem.at[slot, half * 3 + k - 1],
            recv_sem=xr_sem.at[slot, half * 3 + k - 1],
            device_id=at(other, yh, yl, z, core),
            device_id_type=MESH,
        )

    def spread(slot, half):
        for k in (2, 1, 3):
            x_copy(slot, half, k).start()

    def product(items, col, cols):
        total = sum(rows for _, _, rows, _ in items)
        at_row = 0
        for slot, row, rows, _ in items:
            a = got[slot, row : row + rows, col : col + cols]
            h = a.astype(jnp.bfloat16)
            both[at_row : at_row + rows, :cols] = h
            low = (a - h.astype(jnp.float32)).astype(jnp.bfloat16)
            both[total + at_row : total + at_row + rows, :cols] = low
            at_row += rows
        for c in range(0, COLS, 256):
            t = thi[col : col + cols, c : c + 256]
            r2 = jnp.dot(both[: 2 * total, :cols], t, preferred_element_type=jnp.float32)
            t = tlo[col : col + cols, c : c + 256]
            r = jnp.dot(both[:total, :cols], t, preferred_element_type=jnp.float32)
            r += r2[:total] + r2[total:]
            at_row = 0
            for slot, row, rows, fresh in items:
                new = r[at_row : at_row + rows]
                if not fresh:
                    new += part[slot, row : row + rows, c : c + 256]
                part[slot, row : row + rows, c : c + 256] = new
                at_row += rows

    done = set()

    def units(blocks, part_):
        product(
            [(slot_of(p), h * BLOCK, BLOCK, (p, h) not in done) for p, h in blocks],
            OFF[part_], SIZE[part_],
        )
        for place, half in blocks:
            if (place, half) in done:
                spread(slot_of(place), half)
            done.add((place, half))

    def block_owner(slot):
        row = (yl + slot // 4) % 2
        ring = (z + slot % 4) % 4
        return row * 2 + ring // 2, ring % 2

    def y_copy(slot, half):
        return pltpu.make_async_remote_copy(
            src_ref=st.at[slot, half],
            dst_ref=ry.at[slot, half],
            send_sem=ys_sem.at[slot, half],
            recv_sem=yr_sem.at[slot, half],
            device_id=opposite,
            device_id_type=MESH,
        )

    def o_copy(slot, half):
        ox, _ = block_owner(slot)
        return pltpu.make_async_remote_copy(
            src_ref=st.at[slot, half],
            dst_ref=ob.at[half, pl.ds(pl.multiple_of(x * STRIP, STRIP), STRIP)],
            send_sem=os_sem.at[slot, half],
            recv_sem=or_sem.at[half, (x + 3 - ox) % 4],
            device_id=at(ox, yh, yl, z, core),
            device_id_type=MESH,
        )

    def sum_x(place, half):
        slot = slot_of(place)
        for k in range(3):
            arrival(rx.at[slot, half, k], xr_sem.at[slot, half * 3 + k])
        start = pl.multiple_of(half * BLOCK + x * STRIP, STRIP)
        own = part[slot, pl.ds(start, STRIP), :]
        st[slot, half] = (own + rx[slot, half, 0]) + (rx[slot, half, 1] + rx[slot, half, 2])

        @pl.when(block_owner(slot)[1] != yh)
        def _():
            y_copy(slot, half).start()

    def sum_y(place, half):
        slot = slot_of(place)
        ox, oyh = block_owner(slot)

        @pl.when(oyh == yh)
        def _():
            arrival(ry.at[slot, half], yr_sem.at[slot, half])
            st[slot, half] = st[slot, half] + ry[slot, half]

            @pl.when(ox == x)
            def _():
                ob[half, pl.ds(pl.multiple_of(x * STRIP, STRIP), STRIP), :] = st[slot, half]

            @pl.when(ox != x)
            def _():
                o_copy(slot, half).start()

    for h in (0, 1):
        mine[h].wait()
        rows = pl.ds(pl.multiple_of(h * BLOCK + HALF - first, HALF), HALF)
        arrival(got.at[0, rows], sib_sem.at[0, h])
    for s in range(DEPTH // STAGE):
        split_stage(s)
        if (s + 1) * STAGE % CHUNK == 0:
            col = (s + 1) * STAGE - CHUNK
            product([(0, 0, ROWS, col == 0)], col, CHUNK)
    for h in (0, 1):
        spread(0, h)

    for number, group in enumerate(ARRIVALS):
        for place, half, t, ranges in group:
            for rows in ranges:
                arrived(recv_sem, place, half, t, first, rows)
                ref = window(place, half, t, first, rows)
                forward(ref, ref, sib_sem.at[slot_of(place), which(half, t, rows)])
        for link, place, half, t, rows, there in RELAYS.get(number, []):
            send(window(place, half, t, first, rows), link, there, half, t, rows)
        for t in (1, 0):
            blocks = [(place, half) for place, half, t_, _ in group if t_ == t]
            for place, half, t_, ranges in group:
                for rows in ranges if t_ == t else ():
                    arrived(sib_sem, place, half, t, HALF - first, rows)
            if blocks:
                units(blocks, t)
        for place, half in SUM_X.get(number, []):
            sum_x(place, half)
        for place, half in SUM_Y.get(number, []):
            sum_y(place, half)

    sum_x((0, 2), 0)
    sum_y((1, 1), 1)
    sum_x((0, 2), 1)
    sum_y((1, 3), 1)
    sum_y((1, 2), 0)
    sum_x((1, 2), 1)
    sum_y((0, 2), 0)
    sum_y((0, 2), 1)
    sum_y((1, 2), 1)

    for h in (0, 1):
        for k in range(3):
            other = pl.multiple_of((x + 1 + k) % 4 * STRIP, STRIP)
            arrival(ob.at[h, pl.ds(other, STRIP)], or_sem.at[h, k])
        for c in (0, 1):
            row = c * BLOCK + h * HALF
            o_ref[row : row + HALF, :] = ob[h, c * HALF : (c + 1) * HALF, :]

    for copy in started:
        copy.wait_send()
    for slot in range(SLOTS):
        ox, oyh = block_owner(slot)
        for h in (0, 1):
            for k in (1, 2, 3):
                x_copy(slot, h, k).wait_send()

            @pl.when(oyh != yh)
            def _():
                y_copy(slot, h).wait_send()

            @pl.when((oyh == yh) & (ox != x))
            def _():
                o_copy(slot, h).wait_send()


def shards(integrals, amplitudes, vir_energy, occ_energy):
    f32, bf16, dma = jnp.float32, jnp.bfloat16, pltpu.SemaphoreType.DMA
    ladder = pl.pallas_call(
        kernel,
        out_shape=jax.ShapeDtypeStruct((ROWS, COLS), f32),
        in_specs=[pl.BlockSpec(memory_space=pl.ANY)] * 2,
        out_specs=pl.BlockSpec(memory_space=pltpu.VMEM),
        scratch_shapes=[
            pltpu.VMEM((SLOTS, ROWS, DEPTH), f32),
            pltpu.VMEM((DEPTH, COLS), bf16),
            pltpu.VMEM((DEPTH, COLS), bf16),
            pltpu.VMEM((BUFS, STAGE, COLS), f32),
            pltpu.VMEM((SLOTS, ROWS, COLS), f32),
            pltpu.VMEM((SLOTS, 2, 3, STRIP, COLS), f32),
            pltpu.VMEM((SLOTS, 2, STRIP, COLS), f32),
            pltpu.VMEM((SLOTS, 2, STRIP, COLS), f32),
            pltpu.VMEM((2, BLOCK, COLS), f32),
            pltpu.VMEM((6 * BLOCK, SIZE[0]), bf16),
            dma((BUFS,)),
            dma((2,)),
            dma((32,)),
            dma((SLOTS, 8)),
            dma((40,)),
            dma((SLOTS, 8)),
            dma((SLOTS, 6)),
            dma((SLOTS, 6)),
            dma((SLOTS, 2)),
            dma((SLOTS, 2)),
            dma((SLOTS, 2)),
            dma((2, 3)),
        ],
        compiler_params=pltpu.CompilerParams(
            collective_id=0, has_side_effects=True, vmem_limit_bytes=60 << 20
        ),
        name="ladder",
    )(integrals, amplitudes)
    return ladder / (occ_energy[None, :] - vir_energy[:, None])


def solution(mesh):
    return jax.shard_map(
        shards,
        mesh=mesh,
        in_specs=(P("op", "vc"), P("vc", "op"), P("vc"), P("op")),
        out_specs=P("vc", "op"),
        check_vma=False,
    )
```

profile of v0, /device:TPU:6, one launch (start us, length us, event | category | flops | bytes accessed | tf_op | source)
XLA Modules:
  0.0 96.1 jit_solution(7282022287542865332)
XLA Ops:
  0.0 0.0 copy-start
  0.0 0.0 copy-start.1
  0.0 94.1 %ladder.1 = f32[128,1024]{1,0:T(8,128)} custom-call(f32[64,4096]{1,0:T(8,128)} %i_hbm.1, f32[4096,1024]{1,0:T(8,128)} %t_hbm.1), custom_call_target="tpu_custom_call" | custom-call | tf_op jit(solution)/shard_map/ladder/pallas_call | solution.py:380
  94.1 0.0 copy-done
  94.1 0.0 copy-done.1
  94.1 2.0 %subtract_divide_fusion = f32[128,1024]{1,0:T(8,128)} fusion(f32[128,1024]{1,0:T(8,128)} %ladder.1, f32[128]{0:T(128)S(1)} %copy-done.1, f32[1024]{0:T(1024)S(1)} %copy-done), kind=kLoop, calls=%fused_computation | loop fusion | flops 262144 | bytes 1053184 | tf_op jit(solution)/shard_map/div | solution.py:414
Async XLA Ops:
  0.0 94.1 %copy-start = (f32[1024]{0:T(1024)S(1)}, f32[1024]{0:T(1024)}, u32[]{:S(2)}) copy-start(f32[1024]{0:T(1024)} %param.7) | copy-start | bytes 12292
  0.0 94.1 %copy-start.1 = (f32[128]{0:T(128)S(1)}, f32[128]{0:T(128)}, u32[]{:S(2)}) copy-start(f32[128]{0:T(128)} %param.6) | copy-start | bytes 1540
where the time goes:
time: 96.8 us; the launch traced here: 96.1 us
  Pallas kernels  94.1 us (97%)
  other arithmetic  1.98 us (2%)
    pallas_call x1, Pallas kernels, shards(): pl.pallas_call(kernel, out_shape=jax.ShapeDtypeStruct((ROWS, COLS), f32),...  94.1 us
    div x1, other arithmetic, shards(): return ladder / (occ_energy[None, :] - vir_energy[:, None])  1.98 us

commit v1 on v0

--- a/solution.py
+++ b/solution.py
@@ -67,6 +67,8 @@
     9: halves(1, (1, 1)),
     10: [((1, 3), 1), ((1, 2), 0)],
 }
+PRE_X = {11: halves(0, (0, 2))}
+PRE_Y = {11: halves(1, (1, 1))}
 SUM_Y = {
     3: [(OWN, 0), (OWN, 1)],
     6: halves(0, *NEAR),
@@ -219,27 +221,37 @@
 
     def product(items, col, cols):
         total = sum(rows for _, _, rows, _ in items)
-        at_row = 0
-        for slot, row, rows, _ in items:
-            a = got[slot, row : row + rows, col : col + cols]
-            h = a.astype(jnp.bfloat16)
-            both[at_row : at_row + rows, :cols] = h
-            low = (a - h.astype(jnp.float32)).astype(jnp.bfloat16)
-            both[total + at_row : total + at_row + rows, :cols] = low
-            at_row += rows
-        for c in range(0, COLS, 256):
-            t = thi[col : col + cols, c : c + 256]
-            r2 = jnp.dot(both[: 2 * total, :cols], t, preferred_element_type=jnp.float32)
-            t = tlo[col : col + cols, c : c + 256]
-            r = jnp.dot(both[:total, :cols], t, preferred_element_type=jnp.float32)
-            r += r2[:total] + r2[total:]
+        step = 1024 if total > BLOCK else cols
+        for start in range(col, col + cols, step):
+            end = min(start + step, col + cols)
+            width = end - start
             at_row = 0
-            for slot, row, rows, fresh in items:
-                new = r[at_row : at_row + rows]
-                if not fresh:
-                    new += part[slot, row : row + rows, c : c + 256]
-                part[slot, row : row + rows, c : c + 256] = new
+            for slot, row, rows, _ in items:
+                a = got[slot, row : row + rows, start:end]
+                h = a.astype(jnp.bfloat16)
+                both[at_row : at_row + rows, :width] = h
+                low = (a - h.astype(jnp.float32)).astype(jnp.bfloat16)
+                both[total + at_row : total + at_row + rows, :width] = low
                 at_row += rows
+            for c in range(0, COLS, 256):
+                t = thi[start:end, c : c + 256]
+                if total > BLOCK:
+                    r = jnp.dot(both[:total, :width], t, preferred_element_type=jnp.float32)
+                    r += jnp.dot(
+                        both[total : 2 * total, :width], t, preferred_element_type=jnp.float32
+                    )
+                else:
+                    r2 = jnp.dot(both[: 2 * total, :width], t, preferred_element_type=jnp.float32)
+                    r = r2[:total] + r2[total:]
+                t = tlo[start:end, c : c + 256]
+                r += jnp.dot(both[:total, :width], t, preferred_element_type=jnp.float32)
+                at_row = 0
+                for slot, row, rows, fresh in items:
+                    new = r[at_row : at_row + rows]
+                    if start > col or not fresh:
+                        new += part[slot, row : row + rows, c : c + 256]
+                    part[slot, row : row + rows, c : c + 256] = new
+                    at_row += rows
 
     done = set()
 
@@ -328,6 +340,10 @@
                 forward(ref, ref, sib_sem.at[slot_of(place), which(half, t, rows)])
         for link, place, half, t, rows, there in RELAYS.get(number, []):
             send(window(place, half, t, first, rows), link, there, half, t, rows)
+        for place, half in PRE_X.get(number, []):
+            sum_x(place, half)
+        for place, half in PRE_Y.get(number, []):
+            sum_y(place, half)
         for t in (1, 0):
             blocks = [(place, half) for place, half, t_, _ in group if t_ == t]
             for place, half, t_, ranges in group:
@@ -340,8 +356,6 @@
         for place, half in SUM_Y.get(number, []):
             sum_y(place, half)
 
-    sum_x((0, 2), 0)
-    sum_y((1, 1), 1)
     sum_x((0, 2), 1)
     sum_y((1, 3), 1)
     sum_y((1, 2), 0)

time: 96.8 us -> 98.2 us (1.014)
  Pallas kernels: 94.1 us -> 95.6 us
    pallas_call x1, Pallas kernels: 94.1 us -> 95.6 us  [shards(): pl.pallas_call(kernel, out_shape=jax.ShapeDtypeStruct((ROWS, COLS), f32),...]
where the time goes in v1:
time: 98.2 us; the launch traced here: 97.6 us
  Pallas kernels  95.6 us (97%)
  other arithmetic  1.98 us (2%)
    pallas_call x1, Pallas kernels, shards(): pl.pallas_call(kernel, out_shape=jax.ShapeDtypeStruct((ROWS, COLS), f32),...  95.6 us
    div x1, other arithmetic, shards(): return ladder / (occ_energy[None, :] - vir_energy[:, None])  1.98 us

profile of v1, /device:TPU:6, one launch (start us, length us, event | category | flops | bytes accessed | tf_op | source)
XLA Modules:
  0.0 97.6 jit_solution(8626825184932936035)
XLA Ops:
  0.0 0.0 copy-start
  0.0 0.0 copy-start.1
  0.0 95.6 %ladder.1 = f32[128,1024]{1,0:T(8,128)} custom-call(f32[64,4096]{1,0:T(8,128)} %i_hbm.1, f32[4096,1024]{1,0:T(8,128)} %t_hbm.1), custom_call_target="tpu_custom_call" | custom-call | tf_op jit(solution)/shard_map/ladder/pallas_call | solution.py:394
  95.6 0.0 copy-done
  95.6 0.0 copy-done.1
  95.6 2.0 %subtract_divide_fusion = f32[128,1024]{1,0:T(8,128)} fusion(f32[128,1024]{1,0:T(8,128)} %ladder.1, f32[128]{0:T(128)S(1)} %copy-done.1, f32[1024]{0:T(1024)S(1)} %copy-done), kind=kLoop, calls=%fused_computation | loop fusion | flops 262144 | bytes 1053184 | tf_op jit(solution)/shard_map/div | solution.py:428
Async XLA Ops:
  0.0 95.6 %copy-start = (f32[1024]{0:T(1024)S(1)}, f32[1024]{0:T(1024)}, u32[]{:S(2)}) copy-start(f32[1024]{0:T(1024)} %param.7) | copy-start | bytes 12292
  0.0 95.6 %copy-start.1 = (f32[128]{0:T(128)S(1)}, f32[128]{0:T(128)}, u32[]{:S(2)}) copy-start(f32[128]{0:T(128)} %param.6) | copy-start | bytes 1540

commit v2 on v1

--- a/solution.py
+++ b/solution.py
@@ -6,8 +6,8 @@
 from jax.sharding import PartitionSpec as P
 
 MESH = pl.DeviceIdType.MESH
-OFF = (0, 2560)
-SIZE = (2560, 1536)
+OFF = (0, 2304)
+SIZE = (2304, 1792)
 DEPTH = 4096
 CHUNK = 1024
 HALF = 32
@@ -67,8 +67,6 @@
     9: halves(1, (1, 1)),
     10: [((1, 3), 1), ((1, 2), 0)],
 }
-PRE_X = {11: halves(0, (0, 2))}
-PRE_Y = {11: halves(1, (1, 1))}
 SUM_Y = {
     3: [(OWN, 0), (OWN, 1)],
     6: halves(0, *NEAR),
@@ -340,10 +338,6 @@
                 forward(ref, ref, sib_sem.at[slot_of(place), which(half, t, rows)])
         for link, place, half, t, rows, there in RELAYS.get(number, []):
             send(window(place, half, t, first, rows), link, there, half, t, rows)
-        for place, half in PRE_X.get(number, []):
-            sum_x(place, half)
-        for place, half in PRE_Y.get(number, []):
-            sum_y(place, half)
         for t in (1, 0):
             blocks = [(place, half) for place, half, t_, _ in group if t_ == t]
             for place, half, t_, ranges in group:
@@ -356,6 +350,8 @@
         for place, half in SUM_Y.get(number, []):
             sum_y(place, half)
 
+    sum_x((0, 2), 0)
+    sum_y((1, 1), 1)
     sum_x((0, 2), 1)
     sum_y((1, 3), 1)
     sum_y((1, 2), 0)

time: 98.2 us -> 98.8 us (level)
  Pallas kernels: 95.6 us -> 96.6 us
    pallas_call x1, Pallas kernels: 95.6 us -> 96.6 us  [shards(): pl.pallas_call(kernel, out_shape=jax.ShapeDtypeStruct((ROWS, COLS), f32),...]
where the time goes in v2:
time: 98.8 us; the launch traced here: 98.6 us
  Pallas kernels  96.6 us (98%)
  other arithmetic  1.98 us (2%)
    pallas_call x1, Pallas kernels, shards(): pl.pallas_call(kernel, out_shape=jax.ShapeDtypeStruct((ROWS, COLS), f32),...  96.6 us
    div x1, other arithmetic, shards(): return ladder / (occ_energy[None, :] - vir_energy[:, None])  1.98 us

profile of v2, /device:TPU:6, one launch (start us, length us, event | category | flops | bytes accessed | tf_op | source)
XLA Modules:
  0.0 98.6 jit_solution(2487950060430355919)
XLA Ops:
  0.0 0.0 copy-start
  0.0 0.0 copy-start.1
  0.0 96.6 %ladder.1 = f32[128,1024]{1,0:T(8,128)} custom-call(f32[64,4096]{1,0:T(8,128)} %i_hbm.1, f32[4096,1024]{1,0:T(8,128)} %t_hbm.1), custom_call_target="tpu_custom_call" | custom-call | tf_op jit(solution)/shard_map/ladder/pallas_call | solution.py:390
  96.6 0.0 copy-done
  96.6 0.0 copy-done.1
  96.6 2.0 %subtract_divide_fusion = f32[128,1024]{1,0:T(8,128)} fusion(f32[128,1024]{1,0:T(8,128)} %ladder.1, f32[128]{0:T(128)S(1)} %copy-done.1, f32[1024]{0:T(1024)S(1)} %copy-done), kind=kLoop, calls=%fused_computation | loop fusion | flops 262144 | bytes 1053184 | tf_op jit(solution)/shard_map/div | solution.py:424
Async XLA Ops:
  0.0 96.6 %copy-start = (f32[1024]{0:T(1024)S(1)}, f32[1024]{0:T(1024)}, u32[]{:S(2)}) copy-start(f32[1024]{0:T(1024)} %param.7) | copy-start | bytes 12292
  0.0 96.6 %copy-start.1 = (f32[128]{0:T(128)S(1)}, f32[128]{0:T(128)}, u32[]{:S(2)}) copy-start(f32[128]{0:T(128)} %param.6) | copy-start | bytes 1540
